TPU v7x, 128 devices: a whole 4x4x4 slice. The times are simulated.
128 devices in a mesh: lon: 16 (over y_hi, x, core), lat: 8 (over y_lo, z).
Axes of the slice: x: 4, y: 4 (y_hi: 2, y_lo: 2; y = y_hi * 2 + y_lo), z: 4, core: 2. Of those that a mesh axis runs over, the one named last changes fastest.
Arguments:
- grid_state: bfloat16 [1024, 256, 384], P('lon', 'lat'), may hold values from -6 to 6
- conv_weight: bfloat16 [9, 384, 384], replicated, may hold values from -0.109375 to 0.109375
- mix_weight: bfloat16 [384, 384], replicated, may hold values from -0.3125 to 0.3125
- teacher: bfloat16 [8, 128, 256, 384], P('lat', 'lon'), may hold values from -6 to 6
- tile_mask: int32 [16, 8, 8], P('lon', 'lat'), may hold values from 0 to 1, as said below
- source_owner: int32 [8, 16, 16], P('lat'), may hold values from 0 to 15, as said below
- source_block: int32 [8, 16, 16], P('lat'), may hold values from 0 to 7
- margin_weight: float32 [8, 16, 16], P('lat', 'lon'), may hold values from 0.2 to 1
Outputs:
- next_state: bfloat16 [1024, 256, 384], P('lon', 'lat')
- misfit: bfloat16 [1024, 256, 384], P('lon', 'lat')
- grad_conv: float32 [9, 384, 384], replicated
- grad_mix: float32 [384, 384], replicated
Inputs may be any that keep to these rules, and one draw needn't show every extreme that they name: `tile_mask`: 1 marks an ocean tile; every device holds 1 to 4 ocean tiles, and some device holds exactly 4. `source_owner`: blocks lie in the tile's own latitude row. Among the 16 entries of one device no lon index appears more than 2 times, and on every device some lon index appears exactly 2 times.
All inputs are finite; a program needn't handle non-finite values.
Results may differ from a plain program's by a relative error of at most 0.0032.
Values may be sent and summed in bfloat16 or wider, within the bound.
A program may use at most 128 MiB of HBM per device.

v0:
```python
import math
import jax
import jax.numpy as jnp
from jax import lax
from jax.sharding import PartitionSpec as P

TS = 16
K = 2


def with_halo(cells, sides, width, closed):
    for axis, dim in sides:
        count = lax.axis_size(axis)
        ends = count if closed else count - 1
        head = lax.slice_in_dim(cells, 0, width, axis=dim)
        tail = lax.slice_in_dim(cells, cells.shape[dim] - width, cells.shape[dim], axis=dim)
        cells = jnp.concatenate(
            [
                lax.ppermute(tail, axis, [(i, (i + 1) % count) for i in range(ends)]),
                cells,
                lax.ppermute(head, axis, [((i + 1) % count, i) for i in range(ends)]),
            ],
            axis=dim,
        )
    return cells


def block_step(windows, centre, target, keep_rows, conv_weight, mix_weight, scale):
    count, height, breadth, chans = windows.shape
    height = height - 2
    breadth = breadth - 2
    row_count = count * height * breadth

    def shifted(offset):
        step_lon, step_lat = divmod(offset, 3)
        return windows[:, step_lon : step_lon + height, step_lat : step_lat + breadth, :].reshape(
            row_count, chans
        )

    pre = jnp.zeros((row_count, chans), jnp.float32)
    for offset in range(9):
        pre = pre + jnp.dot(
            shifted(offset), conv_weight[offset], preferred_element_type=jnp.float32
        )
    sigmoid_pre = jax.nn.sigmoid(pre)
    hidden = (pre * sigmoid_pre).astype(jnp.bfloat16)
    full_state = centre.astype(jnp.float32) + jnp.dot(
        hidden, mix_weight, preferred_element_type=jnp.float32
    )
    next_state = (keep_rows * full_state).astype(jnp.bfloat16)
    error = keep_rows * (full_state - target)
    misfit = error.astype(jnp.bfloat16)
    scaled = (error * scale).astype(jnp.bfloat16)
    grad_mix = lax.dot_general(
        hidden, scaled, (((0,), (0,)), ((), ())), preferred_element_type=jnp.float32
    )
    back_grad = lax.dot_general(
        scaled, mix_weight, (((1,), (1,)), ((), ())), preferred_element_type=jnp.float32
    )
    dpre = (back_grad * sigmoid_pre * (1.0 + pre * (1.0 - sigmoid_pre))).astype(jnp.bfloat16)
    grad_conv = jnp.stack(
        [
            lax.dot_general(
                shifted(offset), dpre, (((0,), (0,)), ((), ())), preferred_element_type=jnp.float32
            )
            for offset in range(9)
        ]
    )
    return (next_state, misfit, grad_conv, grad_mix)


def tiles_to_block(tiles, tiles_lon, tiles_lat, side):
    chans = tiles.shape[-1]
    shaped = tiles.reshape(tiles_lon, tiles_lat, side, side, chans)
    return jnp.transpose(shaped, (0, 2, 1, 3, 4)).reshape(tiles_lon * side, tiles_lat * side, chans)


def body(
    grid_state,
    conv_weight,
    mix_weight,
    teacher,
    tile_mask,
    source_owner,
    source_block,
    margin_weight,
):
    lon_count = lax.axis_size("lon")
    lat_count = lax.axis_size("lat")
    my_lon = lax.axis_index("lon")
    width_lon, width_lat, chans = grid_state.shape
    side = TS
    tiles_lon = width_lon // side
    tiles_lat = width_lat // side
    tile_count = tiles_lon * tiles_lat
    cells_tile = side * side
    owners = source_owner[0]
    blocks = source_block[0]
    my_owner = lax.dynamic_index_in_dim(owners, my_lon, 0, keepdims=False)
    my_block = lax.dynamic_index_in_dim(blocks, my_lon, 0, keepdims=False)
    local_blocks = teacher[0]
    held = local_blocks.shape[0]
    wanted = my_owner * held + my_block
    piece = lax.all_gather(local_blocks, "lon", axis=0, tiled=True)
    rows_here = jnp.arange(piece.shape[0], dtype=jnp.int32)
    pick_rows = (wanted[:, None] == rows_here[None, :]).astype(jnp.bfloat16)
    picked = jnp.einsum("rj,jcx->rcx", pick_rows, piece, preferred_element_type=jnp.float32)
    weights = margin_weight[0, 0]
    mixed = picked * weights[:, None, None]
    target_tiles = jnp.sum(mixed.reshape(tile_count, K, cells_tile, chans), axis=1)
    lon_wide = with_halo(grid_state, (("lon", 0),), 1, True)
    padded = with_halo(lon_wide, (("lat", 1),), 1, False)
    scale = 1.0 / math.sqrt(width_lon * lon_count * width_lat * lat_count)
    ocean_tiles = tile_mask[0, 0]
    ocean_grid = ocean_tiles.astype(jnp.float32).reshape(tiles_lon, tiles_lat)
    keep_rows = jnp.broadcast_to(
        ocean_grid[:, None, :, None], (tiles_lon, side, tiles_lat, side)
    ).reshape(width_lon * width_lat, 1)
    target_rows = tiles_to_block(target_tiles, tiles_lon, tiles_lat, side).reshape(
        width_lon * width_lat, chans
    )
    next_rows, misfit_rows, grad_conv, grad_mix = block_step(
        padded[None],
        grid_state.reshape(width_lon * width_lat, chans),
        target_rows,
        keep_rows,
        conv_weight,
        mix_weight,
        scale,
    )
    next_state = next_rows.reshape(width_lon, width_lat, chans)
    misfit = misfit_rows.reshape(width_lon, width_lat, chans)
    grad_conv, grad_mix = lax.psum((grad_conv, grad_mix), ("lon", "lat"))
    return (next_state, misfit, grad_conv, grad_mix)


def solution(mesh):
    in_specs = (
        P("lon", "lat", None),
        P(),
        P(),
        P("lat", "lon", None, None),
        P("lon", "lat", None),
        P("lat", None, None),
        P("lat", None, None),
        P("lat", "lon", None),
    )
    out_specs = (P("lon", "lat", None), P("lon", "lat", None), P(), P())
    return jax.shard_map(body, mesh=mesh, in_specs=in_specs, out_specs=out_specs, check_vma=False)
```

profile of v0, /device:TPU:1, one launch (start us, length us, event | category | flops | bytes accessed | tf_op | source)
XLA Modules:
  0.0 406.9 jit_solution(4890446071105545086)
XLA Ops:
  7.2 3.6 copy.15
  11.5 1.4 collective-permute-start.1
  13.0 1.2 collective-permute-start
  14.2 4.4 %collective-permute-done = bf16[1,32,384]{2,1,0:T(8,128)(2,1)S(1)} collective-permute-done((bf16[1,32,384]{2,1,0:T(8,128)(2,1)S(1)}, bf16[1,32,384]{2,1,0:T(8,128)(2,1)S(1)}, u32[]{:S(2)}, u32[]{:S(2)}) %collective-permute-start) | collective-permute-done | bytes 24608 | tf_op jit(solution)/shard_map/ppermute | solution.py:19
  19.1 3.5 collective-permute-start.2
  22.6 1.3 collective-permute-start.3
  25.0 3.2 collective-permute-done.3
  28.2 1.3 maximum_bitcast_fusion
  29.5 4.9 %fusion.48 = (bf16[1,64,32,384]{3,2,1,0:T(8,128)(2,1)}, bf16[1,64,32,384]{3,2,1,0:T(8,128)(2,1)S(1)}, bf16[1,64,32,384]{3,2,1,0:T(8,128)(2,1)S(1)}, bf16[1,64,32...) fusion(bf16[1,66,34,384]{3,2,1,0:T(8,128)(2,1)S(1)} %maximum_bi, ...), kind=kLoop, calls=%fused_computation.69 | loop fusion | bytes 28311552 | tf_op jit(solution)/shard_map/slice | solution.py:36
  34.5 2.5 fusion.16
  37.0 1.5 copy-done.19
  40.7 1.1 fusion.22
  46.6 4.9 %add_add_fusion = f32[2048,384]{1,0:T(8,128)} fusion(f32[2048,384]{1,0:T(8,128)S(1)} %fusion.16, f32[2048,384]{1,0:T(8,128)S(1)} %fusion.18, f32[2048,384]{1,0:T(8,128)S(1)} %fusion.20, f32[2048,384]{1,0:T(8,128)S(1)} %fusion.22, f32[2048,384]{1,0:T(8,128)S(1)} %fusion.24, f32[2048,384]{1,0:T(8,128)S(1)} %fusion.26, f32[2048,384]{1,0:T(8,128)S(1)} %fusion.30, ...), kind=kOutput, calls=%fused_computation.11 | convolution fusion | flops 610271232 | bytes 30179328 | tf_op jit(solution)/shard_map/dot_general | solution.py:42
  51.5 129.9 %all-gather.3.cloned.1.call-done = bf16[1,128,256,384]{3,1,2,0:T(8,128)(2,1)} async-done(((bf16[1,8,256,384]{3,1,2,0:T(8,128)(2,1)}), bf16[1,128,256,384]{3,1,2,0:T(8,128)(2,1)}) %all-gather.3.cloned.1.call-update) | async-done | bytes 25165840 | tf_op jit(solution)/shard_map/all_gather | solution.py:104
  181.4 12.9 %broadcast_multiply_fusion = f32[16,256,384]{2,0,1:T(8,128)} fusion(f32[16]{0:T(128)S(1)} %bitcast.148, bf16[1,128,256,384]{3,1,2,0:T(8,128)(2,1)} %all-gather.3.cloned.1.call-done, s32[16]{0:T(128)S(1)} %add_bitcast_fusion), kind=kOutput, calls=%fused_computation.7 | convolution fusion | flops 404228096 | bytes 31457408 | tf_op jit(solution)/shard_map/rj,jcx->rcx/dot_general | solution.py:107
  194.3 8.2 %reshape.95 = f32[8,2,256,384]{3,1,0,2:T(2,128)} reshape(f32[16,256,384]{2,0,1:T(8,128)} %broadcast_multiply_fusion) | data formatting | bytes 12582912 | tf_op jit(solution)/shard_map/reshape | solution.py:110
  202.5 10.3 %reduce_sum.9 = f32[8,256,384]{2,0,1:T(8,128)S(1)} reduce(f32[8,2,256,384]{3,1,0,2:T(2,128)} %reshape.95, f32[]{:T(128)} %constant.22.clone.1), dimensions={1}, to_apply=%region_0.1 | reduce | flops 786432 | bytes 9437188 | tf_op jit(solution)/shard_map/reduce_sum | solution.py:110
  213.8 1.4 copy-done.18
  215.7 3.2 fusion.46
  218.9 1.9 fusion.14
  220.8 1.8 multiply_convert_fusion
  222.6 1.8 fusion.13
  224.4 1.8 fusion.12
  226.2 1.8 fusion.11
  228.1 1.8 fusion.10
  229.9 1.8 fusion.9
  231.8 1.8 fusion.8
  233.6 1.8 fusion.7
  235.4 1.8 fusion.6
  237.2 1.8 fusion.5
  239.1 154.6 %all-reduce.3.cloned.1.call-done = (f32[9,384,384]{2,1,0:T(8,128)}, f32[384,384]{1,0:T(8,128)}) async-done(((f32[9,384,384]{2,1,0:T(8,128)}, f32[384,384]{1,0:T(8,128)}), (f32[9,384,384]{2,1,0:T(8,128)}, f32[384,384]{1,0:T(8,128)})) %all-reduce.3.cloned.1.call-update) | async-done | bytes 5898256 | tf_op jit(solution)/shard_map/psum | solution.py:133
  393.7 5.3 %copy.30 = f32[9,384,384]{2,1,0:T(8,128)} copy(f32[9,384,384]{2,1,0:T(8,128)} %get-tuple-element.24) | data formatting | bytes 10616832
  (73 shorter events, 11.6 us)
Async XLA Ops:
  7.2 206.7 %copy-start = (bf16[384,384]{1,0:T(8,128)(2,1)S(1)}, bf16[384,384]{1,0:T(8,128)(2,1)}, u32[]{:S(2)}) copy-start(bf16[384,384]{1,0:T(8,128)(2,1)} %param.10) | copy-start | bytes 884740
  7.2 3.7 copy-start.20
  7.2 7.0 %copy-start.24 = (s32[1,1,8]{2,1,0:T(1,128)S(1)}, s32[1,1,8]{2,1,0:T(1,128)}, u32[]{:S(2)}) copy-start(s32[1,1,8]{2,1,0:T(1,128)} %param.12) | copy-start | bytes 100
  7.2 174.2 %all-gather.3.cloned.1.call-start = ((), (), s32[]{:S(2)}) async-start(), calls=%async_computation | async-start | bytes 26738688 | tf_op jit(solution)/shard_map/all_gather | solution.py:104
  10.9 382.8 %all-reduce.3.cloned.1.call-start = ((), (), s32[]{:S(2)}) async-start(), calls=%async_computation.1 | async-start | bytes 11796480 | tf_op jit(solution)/shard_map/psum | solution.py:133
  11.5 7.3 %collective-permute-start.1 = (bf16[1,32,384]{2,1,0:T(8,128)(2,1)}, bf16[1,32,384]{2,1,0:T(8,128)(2,1)S(1)}, u32[]{:S(2)}, u32[]{:S(2)}) collective-permute-start(bf16[1,32,384]{2,1,0:T(8,128)(2,1)} %get-tuple-element.20), channel_id=1, source_target_pairs={{8,0},{16,8},{24,16},{32,24},{40,32},{48,40},{56,48},{64,56},{72,6... | collective-permute-start | bytes 73736 | tf_op jit(solution)/shard_map/ppermute | solution.py:21
  13.0 5.6 %collective-permute-start = (bf16[1,32,384]{2,1,0:T(8,128)(2,1)S(1)}, bf16[1,32,384]{2,1,0:T(8,128)(2,1)S(1)}, u32[]{:S(2)}, u32[]{:S(2)}) collective-permute-start(bf16[1,32,384]{2,1,0:T(8,128)(2,1)S(1)} %get-tuple-element.21), channel_id=1, source_target_pairs={{0,8},{8,16},{16,24},{24,32},{32,40},{40,48},{48,56},{56,64},{64,7... | collective-permute-start | bytes 73736 | tf_op jit(solution)/shard_map/ppermute | solution.py:19
  19.1 5.9 %collective-permute-start.2 = (bf16[66,1,384]{2,1,0:T(2,128)(2,1)S(1)}, bf16[66,1,384]{2,1,0:T(2,128)(2,1)S(1)}, u32[]{:S(2)}, u32[]{:S(2)}) collective-permute-start(bf16[66,1,384]{2,1,0:T(2,128)(2,1)S(1)} %get-tuple-element.18), channel_id=1, source_target_pairs={{0,1},{1,2},{2,3},{3,4},{4,5},{5,6},{6,7},{8,9},{9,10},{10,11},{11... | collective-permute-start | bytes 152072 | tf_op jit(solution)/shard_map/ppermute | solution.py:19
  22.6 5.6 %collective-permute-start.3 = (bf16[66,1,384]{2,1,0:T(2,128)(2,1)S(1)}, bf16[66,1,384]{2,1,0:T(2,128)(2,1)S(1)}, u32[]{:S(2)}, u32[]{:S(2)}) collective-permute-start(bf16[66,1,384]{2,1,0:T(2,128)(2,1)S(1)} %get-tuple-element.19), channel_id=1, source_target_pairs={{1,0},{2,1},{3,2},{4,3},{5,4},{6,5},{7,6},{9,8},{10,9},{11,10},{12... | collective-permute-start | bytes 152072 | tf_op jit(solution)/shard_map/ppermute | solution.py:21
  34.4 2.6 copy-start.1
  34.4 2.6 copy-start.3
  34.4 5.2 %copy-start.5 = (bf16[1,64,32,384]{3,2,1,0:T(8,128)(2,1)}, bf16[1,64,32,384]{3,2,1,0:T(8,128)(2,1)S(1)}, u32[]{:S(2)}) copy-start(bf16[1,64,32,384]{3,2,1,0:T(8,128)(2,1)S(1)} %get-tuple-element.12) | copy-start | bytes 4718596
  34.4 6.3 %copy-start.7 = (bf16[1,64,32,384]{3,2,1,0:T(8,128)(2,1)}, bf16[1,64,32,384]{3,2,1,0:T(8,128)(2,1)S(1)}, u32[]{:S(2)}) copy-start(bf16[1,64,32,384]{3,2,1,0:T(8,128)(2,1)S(1)} %get-tuple-element.13) | copy-start | bytes 4718596
  34.4 7.4 %copy-start.9 = (bf16[1,64,32,384]{3,2,1,0:T(8,128)(2,1)}, bf16[1,64,32,384]{3,2,1,0:T(8,128)(2,1)S(1)}, u32[]{:S(2)}) copy-start(bf16[1,64,32,384]{3,2,1,0:T(8,128)(2,1)S(1)} %get-tuple-element.14) | copy-start | bytes 4718596
  34.4 8.5 %copy-start.11 = (bf16[1,64,32,384]{3,2,1,0:T(8,128)(2,1)}, bf16[1,64,32,384]{3,2,1,0:T(8,128)(2,1)S(1)}, u32[]{:S(2)}) copy-start(bf16[1,64,32,384]{3,2,1,0:T(8,128)(2,1)S(1)} %get-tuple-element.15) | copy-start | bytes 4718596
  34.4 9.6 %copy-start.13 = (bf16[1,64,32,384]{3,2,1,0:T(8,128)(2,1)}, bf16[1,64,32,384]{3,2,1,0:T(8,128)(2,1)S(1)}, u32[]{:S(2)}) copy-start(bf16[1,64,32,384]{3,2,1,0:T(8,128)(2,1)S(1)} %get-tuple-element.16) | copy-start | bytes 4718596
  34.4 4.0 copy-start.19
  44.1 1.4 copy-start.15
  46.6 134.8 %copy-start.23 = (f32[1,1,16]{2,1,0:T(1,128)S(1)}, f32[1,1,16]{2,1,0:T(1,128)}, u32[]{:S(2)}) copy-start(f32[1,1,16]{2,1,0:T(1,128)} %param.15) | copy-start | bytes 196
  213.3 1.9 copy-start.18
  213.4 2.3 copy-start.21
  220.8 1.8 copy-start.16
  222.6 1.8 copy-start.14
  224.4 1.8 copy-start.12
  226.2 1.8 copy-start.10
  228.1 1.8 copy-start.8
  229.9 1.8 copy-start.6
  231.7 1.8 copy-start.4
  233.6 1.8 copy-start.2
  235.4 1.8 copy-start.17
  393.7 5.3 %copy-start.22 = (f32[384,384]{1,0:T(8,128)S(1)}, f32[384,384]{1,0:T(8,128)}, u32[]{:S(2)}) copy-start(f32[384,384]{1,0:T(8,128)} %get-tuple-element.25) | copy-start | bytes 1769476
Sparse Core Ops, SparseCore 0:
  11.0 170.3 all-gather.2
  239.2 154.4 all-reduce.2
where the time goes:
time: 412 us; the launch traced here: 407 us
  waiting for transfers between devices  292 us (71%)
  matrix products  51.3 us (12%)
  local copies, waits for them, and re-layouts  29 us (7%)
  between operations  14.6 us (4%)
  other arithmetic  12.3 us (3%)
  starting transfers between devices  7.52 us (2%)
    psum x1, waiting for transfers between devices, body(): grad_conv, grad_mix = lax.psum((grad_conv, grad_mix), ('lon', 'lat'))  155 us
    all_gather x1, waiting for transfers between devices, body(): piece = lax.all_gather(local_blocks, 'lon', axis=0, tiled=True)  130 us
    dot_general x9, matrix products, block_step(): lax.dot_general(shifted(offset), dpre, (((0,), (0,)), ((), ())), preferre...  16.4 us
    dot_general x9, matrix products, block_step(): jnp.dot(shifted(offset), conv_weight[offset], preferred_element_type=jnp....  15.1 us
    unnamed x55, local copies, waits for them, and re-layouts  13.8 us
    dot_general x1, matrix products, body(): jnp.einsum('rj,jcx->rcx', pick_rows, piece, preferred_element_type=jnp.fl...  12.9 us
    reduce_sum x1, other arithmetic, body(): jnp.sum(mixed.reshape(tile_count, K, cells_tile, chans), axis=1)  10.3 us
  transfers between devices with their start and end apart: 6, of which 4 were waited for; matrix products, arithmetic and copies ran while one was open for 6% of the time, Pallas kernels for 0%

commit v1 on v0

--- a/solution.py
+++ b/solution.py
@@ -1,3 +1,4 @@
+import functools
 import math
 import jax
 import jax.numpy as jnp
@@ -6,6 +7,15 @@
 
 TS = 16
 K = 2
+
+
+def apply_wall(inner_x, ax_name, lane_axis):
+    for no in (ax_name, lane_axis):
+        inner_x = jax.lax.psum(inner_x, axis_name=no)
+    return inner_x
+
+
+_fix_cube = functools.partial(apply_wall, ax_name="lon", lane_axis="lat")
 
 
 def with_halo(cells, sides, width, closed):
@@ -130,7 +140,7 @@
     )
     next_state = next_rows.reshape(width_lon, width_lat, chans)
     misfit = misfit_rows.reshape(width_lon, width_lat, chans)
-    grad_conv, grad_mix = lax.psum((grad_conv, grad_mix), ("lon", "lat"))
+    grad_conv, grad_mix = _fix_cube((grad_conv, grad_mix))
     return (next_state, misfit, grad_conv, grad_mix)
 
 

time: 412 us -> 552 us (1.34)
  waiting for transfers between devices: 292 us -> 432 us
    psum x1 -> x2, waiting for transfers between devices: 155 us -> 295 us  [apply_wall(): inner_x = jax.lax.psum(inner_x, axis_name=no)]
  transfers between devices with their start and end apart: 6 -> 7, of which waited for: 4 -> 5; matrix products, arithmetic and copies ran while one was open for 6% -> 4% of each run, Pallas kernels for 0% -> 0%
where the time goes in v1:
time: 552 us; the launch traced here: 547 us
  waiting for transfers between devices  432 us (78%)
  matrix products  51.3 us (9%)
  local copies, waits for them, and re-layouts  29 us (5%)
  between operations  14.3 us (3%)
  other arithmetic  12.3 us (2%)
  starting transfers between devices  7.56 us (1%)
    psum x2, waiting for transfers between devices, apply_wall(): inner_x = jax.lax.psum(inner_x, axis_name=no)  295 us
    all_gather x1, waiting for transfers between devices, body(): piece = lax.all_gather(local_blocks, 'lon', axis=0, tiled=True)  130 us
    dot_general x9, matrix products, block_step(): lax.dot_general(shifted(offset), dpre, (((0,), (0,)), ((), ())), preferre...  16.4 us
    dot_general x9, matrix products, block_step(): jnp.dot(shifted(offset), conv_weight[offset], preferred_element_type=jnp....  15.1 us
    unnamed x55, local copies, waits for them, and re-layouts  13.8 us
    dot_general x1, matrix products, body(): jnp.einsum('rj,jcx->rcx', pick_rows, piece, preferred_element_type=jnp.fl...  12.9 us
  transfers between devices with their start and end apart: 7, of which 5 were waited for; matrix products, arithmetic and copies ran while one was open for 4% of the time, Pallas kernels for 0%

profile of v1, /device:TPU:1, one launch (start us, length us, event | category | flops | bytes accessed | tf_op | source)
XLA Modules:
  0.0 546.9 jit_solution(13987316191382114208)
XLA Ops:
  7.2 3.6 copy.15
  11.5 1.4 collective-permute-start.1
  13.0 1.2 collective-permute-start
  14.2 4.4 collective-permute-done
  19.1 3.5 collective-permute-start.2
  22.6 1.3 collective-permute-start.3
  25.0 3.2 collective-permute-done.3
  28.2 1.3 maximum_bitcast_fusion
  29.5 4.9 fusion.48
  34.5 2.5 fusion.16
  37.0 1.5 copy-done.19
  46.6 4.9 add_add_fusion
  51.5 129.9 %all-gather.3.cloned.1.call-done = bf16[1,128,256,384]{3,1,2,0:T(8,128)(2,1)} async-done(((bf16[1,8,256,384]{3,1,2,0:T(8,128)(2,1)}), bf16[1,128,256,384]{3,1,2,0:T(8,128)(2,1)}) %all-gather.3.cloned.1.call-update) | async-done | bytes 25165840 | tf_op jit(solution)/shard_map/all_gather | solution.py:114
  181.4 12.9 %broadcast_multiply_fusion = f32[16,256,384]{2,0,1:T(8,128)} fusion(f32[16]{0:T(128)S(1)} %bitcast.148, bf16[1,128,256,384]{3,1,2,0:T(8,128)(2,1)} %all-gather.3.cloned.1.call-done, s32[16]{0:T(128)S(1)} %add_bitcast_fusion), kind=kOutput, calls=%fused_computation.7 | convolution fusion | flops 404228096 | bytes 31457408 | tf_op jit(solution)/shard_map/rj,jcx->rcx/dot_general | solution.py:117
  194.3 8.2 %reshape.95 = f32[8,2,256,384]{3,1,0,2:T(2,128)} reshape(f32[16,256,384]{2,0,1:T(8,128)} %broadcast_multiply_fusion) | data formatting | bytes 12582912 | tf_op jit(solution)/shard_map/reshape | solution.py:120
  202.5 10.3 %reduce_sum.9 = f32[8,256,384]{2,0,1:T(8,128)S(1)} reduce(f32[8,2,256,384]{3,1,0,2:T(2,128)} %reshape.95, f32[]{:T(128)} %constant.22.clone.1), dimensions={1}, to_apply=%region_0.1 | reduce | flops 786432 | bytes 9437188 | tf_op jit(solution)/shard_map/reduce_sum | solution.py:120
  213.9 1.4 copy-done.18
  215.7 3.2 fusion.46
  218.9 1.9 fusion.14
  220.8 1.8 multiply_convert_fusion
  222.6 1.8 fusion.13
  224.4 1.8 fusion.12
  226.3 1.8 fusion.11
  228.1 1.8 fusion.10
  229.9 1.8 fusion.9
  231.8 1.8 fusion.8
  233.6 1.8 fusion.7
  235.4 1.8 fusion.6
  237.3 1.8 fusion.5
  239.2 152.5 %all-reduce.5.cloned.1.call-done = (f32[9,384,384]{2,1,0:T(8,128)}, f32[384,384]{1,0:T(8,128)}) async-done(((f32[9,384,384]{2,1,0:T(8,128)}, f32[384,384]{1,0:T(8,128)}), (f32[9,384,384]{2,1,0:T(8,128)}, f32[384,384]{1,0:T(8,128)})) %all-reduce.5.cloned.1.call-update) | async-done | bytes 5898256 | tf_op jit(solution)/shard_map/psum | solution.py:14
  391.7 142.4 %all-reduce.7.cloned.1.call-done = (f32[9,384,384]{2,1,0:T(8,128)}, f32[384,384]{1,0:T(8,128)}) async-done(((f32[9,384,384]{2,1,0:T(8,128)}, f32[384,384]{1,0:T(8,128)}), (f32[9,384,384]{2,1,0:T(8,128)}, f32[384,384]{1,0:T(8,128)})) %all-reduce.7.cloned.1.call-update) | async-done | bytes 5898256 | tf_op jit(solution)/shard_map/psum | solution.py:14
  534.1 5.3 copy.32
  (76 shorter events, 12.8 us)
Async XLA Ops:
  7.2 206.7 %copy-start = (bf16[384,384]{1,0:T(8,128)(2,1)S(1)}, bf16[384,384]{1,0:T(8,128)(2,1)}, u32[]{:S(2)}) copy-start(bf16[384,384]{1,0:T(8,128)(2,1)} %param.10) | copy-start | bytes 884740
  7.2 3.7 copy-start.20
  7.2 7.0 %copy-start.24 = (s32[1,1,8]{2,1,0:T(1,128)S(1)}, s32[1,1,8]{2,1,0:T(1,128)}, u32[]{:S(2)}) copy-start(s32[1,1,8]{2,1,0:T(1,128)} %param.12) | copy-start | bytes 100
  7.2 174.2 %all-gather.3.cloned.1.call-start = ((), (), s32[]{:S(2)}) async-start(), calls=%async_computation | async-start | bytes 26738688 | tf_op jit(solution)/shard_map/all_gather | solution.py:114
  10.9 380.8 %all-reduce.5.cloned.1.call-start = ((), (), s32[]{:S(2)}) async-start(), calls=%async_computation.1 | async-start | bytes 11796480 | tf_op jit(solution)/shard_map/psum | solution.py:14
  11.5 7.3 %collective-permute-start.1 = (bf16[1,32,384]{2,1,0:T(8,128)(2,1)}, bf16[1,32,384]{2,1,0:T(8,128)(2,1)S(1)}, u32[]{:S(2)}, u32[]{:S(2)}) collective-permute-start(bf16[1,32,384]{2,1,0:T(8,128)(2,1)} %get-tuple-element.22), channel_id=1, source_target_pairs={{8,0},{16,8},{24,16},{32,24},{40,32},{48,40},{56,48},{64,56},{72,6... | collective-permute-start | bytes 73736 | tf_op jit(solution)/shard_map/ppermute | solution.py:31
  13.0 5.6 %collective-permute-start = (bf16[1,32,384]{2,1,0:T(8,128)(2,1)S(1)}, bf16[1,32,384]{2,1,0:T(8,128)(2,1)S(1)}, u32[]{:S(2)}, u32[]{:S(2)}) collective-permute-start(bf16[1,32,384]{2,1,0:T(8,128)(2,1)S(1)} %get-tuple-element.23), channel_id=1, source_target_pairs={{0,8},{8,16},{16,24},{24,32},{32,40},{40,48},{48,56},{56,64},{64,7... | collective-permute-start | bytes 73736 | tf_op jit(solution)/shard_map/ppermute | solution.py:29
  19.1 5.9 %collective-permute-start.2 = (bf16[66,1,384]{2,1,0:T(2,128)(2,1)S(1)}, bf16[66,1,384]{2,1,0:T(2,128)(2,1)S(1)}, u32[]{:S(2)}, u32[]{:S(2)}) collective-permute-start(bf16[66,1,384]{2,1,0:T(2,128)(2,1)S(1)} %get-tuple-element.20), channel_id=1, source_target_pairs={{0,1},{1,2},{2,3},{3,4},{4,5},{5,6},{6,7},{8,9},{9,10},{10,11},{11... | collective-permute-start | bytes 152072 | tf_op jit(solution)/shard_map/ppermute | solution.py:29
  22.6 5.6 %collective-permute-start.3 = (bf16[66,1,384]{2,1,0:T(2,128)(2,1)S(1)}, bf16[66,1,384]{2,1,0:T(2,128)(2,1)S(1)}, u32[]{:S(2)}, u32[]{:S(2)}) collective-permute-start(bf16[66,1,384]{2,1,0:T(2,128)(2,1)S(1)} %get-tuple-element.21), channel_id=1, source_target_pairs={{1,0},{2,1},{3,2},{4,3},{5,4},{6,5},{7,6},{9,8},{10,9},{11,10},{12... | collective-permute-start | bytes 152072 | tf_op jit(solution)/shard_map/ppermute | solution.py:31
  34.4 2.6 copy-start.1
  34.4 2.6 copy-start.3
  34.4 5.2 copy-start.5
  34.4 6.3 %copy-start.7 = (bf16[1,64,32,384]{3,2,1,0:T(8,128)(2,1)}, bf16[1,64,32,384]{3,2,1,0:T(8,128)(2,1)S(1)}, u32[]{:S(2)}) copy-start(bf16[1,64,32,384]{3,2,1,0:T(8,128)(2,1)S(1)} %get-tuple-element.15) | copy-start | bytes 4718596
  34.4 7.4 %copy-start.9 = (bf16[1,64,32,384]{3,2,1,0:T(8,128)(2,1)}, bf16[1,64,32,384]{3,2,1,0:T(8,128)(2,1)S(1)}, u32[]{:S(2)}) copy-start(bf16[1,64,32,384]{3,2,1,0:T(8,128)(2,1)S(1)} %get-tuple-element.16) | copy-start | bytes 4718596
  34.4 8.5 %copy-start.11 = (bf16[1,64,32,384]{3,2,1,0:T(8,128)(2,1)}, bf16[1,64,32,384]{3,2,1,0:T(8,128)(2,1)S(1)}, u32[]{:S(2)}) copy-start(bf16[1,64,32,384]{3,2,1,0:T(8,128)(2,1)S(1)} %get-tuple-element.17) | copy-start | bytes 4718596
  34.4 9.6 %copy-start.13 = (bf16[1,64,32,384]{3,2,1,0:T(8,128)(2,1)}, bf16[1,64,32,384]{3,2,1,0:T(8,128)(2,1)S(1)}, u32[]{:S(2)}) copy-start(bf16[1,64,32,384]{3,2,1,0:T(8,128)(2,1)S(1)} %get-tuple-element.18) | copy-start | bytes 4718596
  34.5 4.0 copy-start.19
  44.1 1.4 copy-start.15
  46.6 134.8 %copy-start.23 = (f32[1,1,16]{2,1,0:T(1,128)S(1)}, f32[1,1,16]{2,1,0:T(1,128)}, u32[]{:S(2)}) copy-start(f32[1,1,16]{2,1,0:T(1,128)} %param.15) | copy-start | bytes 196
  213.4 1.9 copy-start.18
  213.4 2.3 copy-start.21
  220.8 1.8 copy-start.16
  222.6 1.8 copy-start.14
  224.4 1.8 copy-start.12
  226.3 1.8 copy-start.10
  228.1 1.8 copy-start.8
  229.9 1.8 copy-start.6
  231.8 1.8 copy-start.4
  233.6 1.8 copy-start.2
  235.4 1.8 copy-start.17
  239.1 295.0 %all-reduce.7.cloned.1.call-start = ((), (), s32[]{:S(2)}) async-start(), calls=%async_computation.2 | async-start | bytes 11796480 | tf_op jit(solution)/shard_map/psum | solution.py:14
  534.1 5.3 copy-start.22
Sparse Core Ops, SparseCore 0:
  11.0 170.3 all-gather.2
  239.2 152.3 all-reduce.4
  394.4 139.6 all-reduce.6
